TPU v7x, 128 devices: a whole 4x4x4 slice. The times are simulated.
128 devices in a mesh: row: 8 (over z, core), col: 16 (over y, x).
Axes of the slice: x: 4, y: 4, z: 4, core: 2. Of those that a mesh axis runs over, the one named last changes fastest.
Arguments:
- snapshots: bfloat16 [4096, 32768], P('row', 'col'), may hold values from -14 to 14
- neighbours: int32 [4096, 128], P('row'), may hold values from 0 to 4095, all different within a row
- start_basis: float32 [32, 4096], replicated, may hold values from -6 to 6
Outputs:
- basis: float32 [32, 4096], P(None, 'row')
- rayleigh: float32 [32, 32], replicated
Inputs may be any that keep to these rules, and one draw needn't show every extreme that they name: `neighbours`: each row names 128 different snapshots.
All inputs are finite; a program needn't handle non-finite values.
Results may differ from a plain program's by a relative error of at most 0.00145.
Values may be sent and summed in bfloat16 or wider, within the bound.
No kernel may reach another device: no remote copies, remote signals or barrier semaphores. Data moves between devices by JAX's collectives and lax.ppermute only.
A program may use at most 128 MiB of HBM per device.

v0:
```python
import math
import jax
import jax.numpy as jnp
from jax import lax
from jax.sharding import PartitionSpec as P

FEATURES = 32768
LAGS = 64
ITERS = 2


def global_sum(value):
    return lax.psum(value, ("row", "col"))


def collect(columns):
    return lax.all_gather(columns, ("row", "col"), axis=1, tiled=True)


def shards(snapshots, neighbours, start_basis):
    row_count = lax.axis_size("row")
    col_count = lax.axis_size("col")
    row_at = lax.axis_index("row")
    col_at = lax.axis_index("col")
    lag_count = LAGS
    whole = lax.all_gather(snapshots, "row", axis=0, tiled=True)
    snap_count = whole.shape[0]
    feat_width = whole.shape[1]
    col_block = snap_count // col_count
    row_block = snapshots.shape[0]
    squares = jnp.sum(jnp.square(whole.astype(jnp.float32)), axis=1)
    padded_rows = jnp.concatenate([jnp.zeros((lag_count, feat_width), whole.dtype), whole], 0)
    padded_norms = jnp.concatenate([jnp.zeros((lag_count,), jnp.float32), squares], 0)
    row_start = row_at * row_block
    ext_rows = lax.dynamic_slice_in_dim(padded_rows, row_start, row_block + lag_count, 0)
    ext_norms = lax.dynamic_slice_in_dim(padded_norms, row_start, row_block + lag_count, 0)
    row_times = row_start - lag_count + jnp.arange(row_block + lag_count, dtype=jnp.int32)
    span = col_block + lag_count
    blocks = whole.reshape(col_count, col_block, feat_width)
    earlier = jnp.concatenate(
        [jnp.zeros((1, lag_count, feat_width), whole.dtype), blocks[:-1, col_block - lag_count :]],
        0,
    )
    source_rows = jnp.concatenate([earlier, blocks], 1).reshape(col_count * span, feat_width)
    norm_blocks = squares.reshape(col_count, col_block)
    norm_earlier = jnp.concatenate(
        [jnp.zeros((1, lag_count), jnp.float32), norm_blocks[:-1, col_block - lag_count :]], 0
    )
    source_norms = jnp.concatenate([norm_earlier, norm_blocks], 1).reshape(col_count * span)
    virtual = jnp.arange(span * lax.axis_size("col"), dtype=jnp.int32)
    times = virtual // span * col_block + virtual % span - lag_count
    inner = lax.dot_general(
        source_rows, ext_rows, (((1,), (1,)), ((), ())), preferred_element_type=jnp.float32
    )
    term = source_norms[:, None] + ext_norms[None, :] - 2.0 * inner
    keep = (times >= 0)[:, None] & (row_times >= 0)[None, :]
    tile = lax.psum_scatter(
        jnp.where(keep, term, 0.0).astype(jnp.bfloat16), "col", scatter_dimension=0, tiled=True
    ).astype(jnp.float32)
    window = 1
    while window < lag_count:
        tile = tile[window:, window:] + tile[:-window, :-window]
        window = window * 2
    lagged = tile[1:, 1:]
    step_rows = math.gcd(row_block, 16)
    block_count = row_block // step_rows
    slot_count = neighbours.shape[1]
    offset = neighbours - col_at * col_block
    inside = (offset >= 0) & (offset < col_block)
    tile_positions = jnp.arange(col_block, dtype=jnp.int32)

    def pick_block(pair):
        offs, lag_rows = pair
        match = offs[:, :, None] == tile_positions[None, None, :]
        return jnp.sum(jnp.where(match, lag_rows[:, None, :], 0.0), axis=2)

    chosen = lax.map(
        pick_block,
        (
            offset.reshape(block_count, step_rows, slot_count),
            lagged.T.reshape(block_count, step_rows, col_block),
        ),
    )
    chosen = chosen.reshape(row_block, slot_count)
    kernel_part = jnp.where(inside, 1.0 / (1.0 + chosen / (LAGS * FEATURES)), 0.0)
    slot_kernel = lax.psum(kernel_part, "col")
    mass = jnp.sum(slot_kernel, axis=1)
    markov = slot_kernel / mass[:, None]
    snap_positions = jnp.arange(snap_count, dtype=jnp.int32)

    def operator_block(pair):
        ids, weights = pair
        match = ids[:, :, None] == snap_positions[None, None, :]
        return jnp.sum(jnp.where(match, weights[:, :, None], 0.0), axis=1)

    transition = lax.map(
        operator_block,
        (
            neighbours.reshape(block_count, step_rows, slot_count),
            markov.reshape(block_count, step_rows, slot_count),
        ),
    )
    transition = transition.reshape(row_block, snap_count)
    piece_width = snap_count // (row_count * col_count)

    def apply_rows(basis_rows):
        return lax.dot_general(
            basis_rows,
            transition,
            (((1,), (1,)), ((), ())),
            precision=lax.Precision.HIGHEST,
            preferred_element_type=jnp.float32,
        )

    def own_piece(image):
        return lax.dynamic_slice_in_dim(image, col_at * piece_width, piece_width, 1)

    basis = start_basis
    for step in range(ITERS):
        piece = own_piece(apply_rows(basis))
        partial_gram = jnp.dot(
            piece, piece.T, precision=lax.Precision.HIGHEST, preferred_element_type=jnp.float32
        )
        gram_small = global_sum(partial_gram) / snap_count
        lower = jnp.linalg.cholesky(gram_small)
        basis = collect(jax.scipy.linalg.solve_triangular(lower, piece, lower=True))
    image_piece = own_piece(apply_rows(basis))
    basis_piece = lax.dynamic_slice_in_dim(
        basis, (row_at * col_count + col_at) * piece_width, piece_width, 1
    )
    partial_ray = jnp.dot(
        basis_piece,
        image_piece.T,
        precision=lax.Precision.HIGHEST,
        preferred_element_type=jnp.float32,
    )
    rayleigh = global_sum(partial_ray) / snap_count
    basis_rows = lax.dynamic_slice_in_dim(basis, row_start, row_block, 1)
    return (basis_rows, rayleigh)


def solution(mesh):
    placed = (P("row", "col"), P("row", None), P())
    return jax.shard_map(
        shards, mesh=mesh, in_specs=placed, out_specs=(P(None, "row"), P()), check_vma=False
    )
```

profile of v0, /device:TPU:1, one launch (start us, length us, event | category | flops | bytes accessed | tf_op | source)
XLA Modules:
  0.0 1007.9 jit_solution(16402256858035387622)
XLA Ops:
  8.0 90.6 %all-gather.2.cloned.1.call-done = bf16[4096,2048]{1,0:T(8,128)(2,1)} async-done(((bf16[512,2048]{1,0:T(8,128)(2,1)}), bf16[4096,2048]{1,0:T(8,128)(2,1)}) %all-gather.2.cloned.1.call-update) | async-done | bytes 16777232 | tf_op jit(solution)/shard_map/all_gather | solution.py:26
  98.6 7.2 multiply_reduce_fusion
  108.7 21.4 %fusion.5 = bf16[16,320,2048]{2,1,0:T(8,128)(2,1)} fusion(bf16[15,64,2048]{2,1,0:T(8,128)(2,1)S(1)} %slice.69, bf16[16,256,2048]{2,1,0:T(8,128)(2,1)} %bitcast.64), kind=kLoop, calls=%fused_computation.15 | loop fusion | flops 62914560 | bytes 41680896 | tf_op jit(solution)/shard_map/concatenate | solution.py:44
  130.2 23.8 %select_convert_fusion = bf16[5120,576]{1,0:T(8,128)(2,1)} fusion(bf16[5120,2048]{1,0:T(8,128)(2,1)} %bitcast.70, f32[576]{0:T(1024)S(1)} %pad_dynamic-slice_fusion.2, f32[5120]{0:T(1024)S(1)} %add.130, pred[576]{0:T(1024)(128)(4,1)S(1)} %add_compare_fusion, pred[5120]{0:T(1024)(128)(4,1)S(1)} %fusion.17, s32[]{:T(128)S(6)} %select_n.56, ...), kind=kOutput, calls=%fused_computation.17 | convolution fusion | flops 12097290240 | bytes 43675460 | tf_op jit(solution)/shard_map/dot_general | solution.py:52
  154.1 80.7 %reduce-scatter.2.cloned.1.call-done = bf16[320,576]{1,0:T(8,128)(2,1)} async-done(((bf16[5120,576]{1,0:T(8,128)(2,1)}), bf16[320,576]{1,0:T(8,128)(2,1)}) %reduce-scatter.2.cloned.1.call-update) | async-done | bytes 368656 | tf_op jit(solution)/shard_map/reduce_scatter | solution.py:57
  238.1 28.1 %while.22 = (s32[]{:T(128)}, f32[32,16,128]{2,1,0:T(8,128)S(1)}, s32[32,16,128]{2,1,0:T(8,128)S(1)}, f32[32,16,256]{2,1,0:T(8,128)S(1)}, s32[]{:T(128)}) while((s32[]{:T(128)}, f32[32,16,128]{2,1,0:T(8,128)S(1)}, s32[32,16,128]{2,1,0:T(8,128)S(1)}, f32[32,16,256]{2,1,0:T(8,128)S(1)}, s32[]{:T(128)}) %tuple.63), condition=%wide.region_4.5_spmd.clone, body=%wide.region_2.4_spmd.clone.sunk | while | flops 1570818 | bytes 98377 | solution.py:77
  267.0 83.3 %all-reduce.6.cloned.1.call-done = f32[512,128]{1,0:T(8,128)} async-done(((f32[512,128]{1,0:T(8,128)}), f32[512,128]{1,0:T(8,128)}) %all-reduce.6.cloned.1.call-update) | async-done | bytes 262160 | tf_op jit(solution)/shard_map/psum | solution.py:86
  352.5 280.2 %while.23 = (s32[]{:T(128)}, f32[32,16,4096]{2,1,0:T(8,128)}, s32[32,16,128]{2,1,0:T(8,128)S(1)}, f32[32,16,128]{2,1,0:T(8,128)S(1)}, s32[]{:T(128)}) while((s32[]{:T(128)}, f32[32,16,4096]{2,1,0:T(8,128)}, s32[32,16,128]{2,1,0:T(8,128)S(1)}, f32[32,16,128]{2,1,0:T(8,128)S(1)}, s32[]{:T(128)}) %tuple.64), condition=%wide.region_9.10_spmd.clone, body=%wide.region_7.9_spmd.clone.sunk | while | flops 25100288 | bytes 836165 | solution.py:96
  352.6 8.0 select_reduce_fusion.6
  361.3 8.0 select_reduce_fusion.6
  370.0 8.0 select_reduce_fusion.6
  378.8 8.0 select_reduce_fusion.6
  387.5 8.0 select_reduce_fusion.6
  396.3 8.0 select_reduce_fusion.6
  405.1 8.0 select_reduce_fusion.6
  413.8 8.0 select_reduce_fusion.6
  422.6 8.0 select_reduce_fusion.6
  431.4 8.0 select_reduce_fusion.6
  440.1 8.0 select_reduce_fusion.6
  448.9 8.0 select_reduce_fusion.6
  457.6 8.0 select_reduce_fusion.6
  466.4 8.0 select_reduce_fusion.6
  475.1 8.0 select_reduce_fusion.6
  483.9 8.0 select_reduce_fusion.6
  492.6 8.0 select_reduce_fusion.6
  501.4 8.0 select_reduce_fusion.6
  510.1 8.0 select_reduce_fusion.6
  518.9 8.0 select_reduce_fusion.6
  527.7 8.0 select_reduce_fusion.6
  536.4 8.0 select_reduce_fusion.6
  545.2 8.0 select_reduce_fusion.6
  553.9 8.0 select_reduce_fusion.6
  562.7 8.0 select_reduce_fusion.6
  571.4 8.0 select_reduce_fusion.6
  580.2 8.0 select_reduce_fusion.6
  589.0 8.0 select_reduce_fusion.6
  597.7 8.0 select_reduce_fusion.6
  606.5 8.0 select_reduce_fusion.6
  615.2 8.0 select_reduce_fusion.6
  623.9 8.0 select_reduce_fusion.6
  632.7 9.2 fusion.46
  642.1 65.8 %psum.29 = f32[32,32]{0,1:T(8,128)S(1)} all-reduce(f32[32,32]{0,1:T(8,128)S(1)} %fusion.36), channel_id=1, replica_groups=mesh['row'=8,'col'=16] {'row','col'}, use_global_device_ids=true, to_apply=%region_10.11 | all-reduce | flops 1024 | bytes 8192 | tf_op jit(solution)/shard_map/psum | solution.py:13
  714.8 63.7 %all_gather.10 = f32[32,4096]{0,1:T(8,128)S(1)} all-gather(f32[32,32]{0,1:T(8,128)S(1)} %fusion.23), channel_id=1, replica_groups=mesh['row'=8,'col'=16] {'row','col'}, dimensions={1}, use_global_device_ids=true | all-gather | bytes 528384 | tf_op jit(solution)/shard_map/all_gather | solution.py:17
  778.6 9.3 fusion.47
  788.1 65.0 %psum.30 = f32[32,32]{0,1:T(8,128)S(1)} all-reduce(f32[32,32]{0,1:T(8,128)S(1)} %fusion.33), channel_id=1, replica_groups=mesh['row'=8,'col'=16] {'row','col'}, use_global_device_ids=true, to_apply=%region_13.16 | all-reduce | flops 1024 | bytes 8192 | tf_op jit(solution)/shard_map/psum | solution.py:13
  860.2 65.1 %all_gather.11 = f32[32,4096]{0,1:T(8,128)S(1)} all-gather(f32[32,32]{0,1:T(8,128)S(1)} %fusion.20), channel_id=1, replica_groups=mesh['row'=8,'col'=16] {'row','col'}, dimensions={1}, use_global_device_ids=true | all-gather | bytes 528384 | tf_op jit(solution)/shard_map/all_gather | solution.py:17
  925.3 9.2 fusion.48
  934.8 65.0 %psum.31 = f32[32,32]{0,1:T(8,128)S(1)} all-reduce(f32[32,32]{0,1:T(8,128)S(1)} %fusion.29), channel_id=1, replica_groups=mesh['row'=8,'col'=16] {'row','col'}, use_global_device_ids=true, to_apply=%region_14.17 | all-reduce | flops 1024 | bytes 8192 | tf_op jit(solution)/shard_map/psum | solution.py:13
  (292 shorter events, 75.8 us)
Async XLA Ops:
  7.2 625.5 %copy-start = (f32[32,4096]{1,0:T(8,128)S(1)}, f32[32,4096]{1,0:T(8,128)}, u32[]{:S(2)}) copy-start(f32[32,4096]{1,0:T(8,128)} %param.12) | copy-start | bytes 1572868
  7.2 91.4 %all-gather.2.cloned.1.call-start = ((), (), s32[]{:S(2)}) async-start(), calls=%async_computation.1 | async-start | bytes 18874368 | tf_op jit(solution)/shard_map/all_gather | solution.py:26
  7.9 226.8 %reduce-scatter.2.cloned.1.call-start = ((), (), s32[]{:S(2)}) async-start(), calls=%async_computation.2 | async-start | bytes 6963200 | tf_op jit(solution)/shard_map/reduce_scatter | solution.py:57
  106.1 24.0 %slice-start = ((s8[16777216]{0:T(1024)(128)(4,1)}), s8[4194304]{0:T(1024)(128)(4,1)S(1)}, s32[]{:S(2)}) async-start(s8[16777216]{0:T(1024)(128)(4,1)} %bitcast.65), calls=%async_computation.4 | async-start | bytes 8388608
  108.7 21.5 %slice-start.1 = ((s8[16777216]{0:T(1024)(128)(4,1)}), s8[4194304]{0:T(1024)(128)(4,1)S(1)}, s32[]{:S(2)}) async-start(s8[16777216]{0:T(1024)(128)(4,1)} %bitcast.65), calls=%async_computation.5 | async-start | bytes 8388608
  108.7 21.4 %slice-start.2 = ((s8[16777216]{0:T(1024)(128)(4,1)}), s8[4194304]{0:T(1024)(128)(4,1)S(1)}, s32[]{:S(2)}) async-start(s8[16777216]{0:T(1024)(128)(4,1)} %bitcast.65), calls=%async_computation.6 | async-start | bytes 8388608
  108.7 21.4 %slice-start.3 = ((s8[16777216]{0:T(1024)(128)(4,1)}), s8[4194304]{0:T(1024)(128)(4,1)S(1)}, s32[]{:S(2)}) async-start(s8[16777216]{0:T(1024)(128)(4,1)} %bitcast.65), calls=%async_computation.7 | async-start | bytes 8388608
  130.1 23.9 %copy-start.1 = (s32[512,128]{1,0:T(8,128)S(1)}, s32[512,128]{1,0:T(8,128)}, u32[]{:S(2)}) copy-start(s32[512,128]{1,0:T(8,128)} %param.11) | copy-start | bytes 786436
  154.0 196.3 %all-reduce.6.cloned.1.call-start = ((), (), s32[]{:S(2)}) async-start(), calls=%async_computation.3 | async-start | bytes 524288 | tf_op jit(solution)/shard_map/psum | solution.py:86
Sparse Core Ops, SparseCore 0:
  9.7 88.8 all-gather.1
  154.1 80.6 reduce-scatter.1
  267.1 83.1 all-reduce.5
where the time goes:
time: 1020 us; the launch traced here: 1010 us
  other arithmetic  330 us (32%)
  blocking collectives  325 us (32%)
  waiting for transfers between devices  255 us (25%)
  matrix products  52.6 us (5%)
  local copies, waits for them, and re-layouts  29.2 us (3%)
  between operations  14.3 us (1%)
    reduce_sum x32, other arithmetic, operator_block(): return jnp.sum(jnp.where(match, weights[:, :, None], 0.0), axis=1)  256 us
    psum x3, blocking collectives, global_sum(): return lax.psum(value, ('row', 'col'))  196 us
    all_gather x2, blocking collectives, collect(): return lax.all_gather(columns, ('row', 'col'), axis=1, tiled=True)  129 us
    all_gather x1, waiting for transfers between devices, shards(): whole = lax.all_gather(snapshots, 'row', axis=0, tiled=True)  90.6 us
    psum x1, waiting for transfers between devices, shards(): slot_kernel = lax.psum(kernel_part, 'col')  83.3 us
    reduce_scatter x1, waiting for transfers between devices, shards(): lax.psum_scatter(jnp.where(keep, term, 0.0).astype(jnp.bfloat16), 'col',...  80.7 us
    dot_general x3, matrix products, apply_rows(): lax.dot_general(basis_rows, transition, (((1,), (1,)), ((), ())), precisi...  27.6 us
    reduce_sum x32, other arithmetic, pick_block(): return jnp.sum(jnp.where(match, lag_rows[:, None, :], 0.0), axis=2)  25.3 us
  transfers between devices with their start and end apart: 3, of which 3 were waited for; matrix products, arithmetic and copies ran while one was open for 0% of the time, Pallas kernels for 0%

commit v1 on v0

--- a/solution.py
+++ b/solution.py
@@ -7,6 +7,12 @@
 FEATURES = 32768
 LAGS = 64
 ITERS = 2
+
+
+def follow_view(a0, dim_i):
+    carry_in = list(a0.shape[1:])
+    carry_in[dim_i] *= a0.shape[0]
+    return jnp.moveaxis(a0, 0, dim_i).reshape(carry_in)
 
 
 def global_sum(value):
@@ -23,7 +29,26 @@
     row_at = lax.axis_index("row")
     col_at = lax.axis_index("col")
     lag_count = LAGS
-    whole = lax.all_gather(snapshots, "row", axis=0, tiled=True)
+    chips = lax.axis_size("row")
+    rows = tuple(((num, (num + 1) % chips) for num in range(chips)))
+    series = tuple(((d, idx) for idx, d in rows))
+    w_next, current_value = ([], [])
+    for dd in range(chips - 1):
+        if dd % 2 == 0:
+            odd = lax.ppermute(w_next[-1] if w_next else snapshots, axis_name="row", perm=rows)
+            w_next.append(odd)
+        else:
+            current_value.append(
+                lax.ppermute(
+                    current_value[-1] if current_value else snapshots, axis_name="row", perm=series
+                )
+            )
+    base_arr = jnp.stack([*w_next[::-1], snapshots, *current_value])
+    val = lax.axis_index("row")
+    block_out = len(w_next)
+    high = val - block_out
+    base_arr = base_arr[(jnp.arange(chips) - high) % chips]
+    whole = follow_view(base_arr, 0)
     snap_count = whole.shape[0]
     feat_width = whole.shape[1]
     col_block = snap_count // col_count

time: 1020 us -> 1080 us (1.059)
  local copies, waits for them, and re-layouts: 29.2 us -> 76.1 us
  starting transfers between devices: 0.12 us -> 14.6 us
    all_gather x1 -> x0, waiting for transfers between devices: 90.6 us -> none  [shards(): whole = lax.all_gather(snapshots, 'row', axis=0, tiled=True)]
    ppermute x0 -> x7, waiting for transfers between devices: none -> 88.6 us  [the longest x4 88.1 us: shards(): lax.ppermute(w_next[-1] if w_next else snapshots, axis_name='row', perm=r...]
    unnamed x14 -> x30, local copies, waits for them, and re-layouts: 1.45 us -> 25.8 us
    gather x0 -> x3, local copies, waits for them, and re-layouts: none -> 22.5 us  [shards(): base_arr = base_arr[(jnp.arange(chips) - high) % chips]]
    ppermute x0 -> x7, starting transfers between devices: none -> 14.4 us  [the longest x4 10.5 us: shards(): lax.ppermute(w_next[-1] if w_next else snapshots, axis_name='row', perm=r...]
  transfers between devices with their start and end apart: 3 -> 9, of which waited for: 3 -> 7; matrix products, arithmetic and copies ran while one was open for 0% -> 1% of each run, Pallas kernels for 0% -> 0%
where the time goes in v1:
time: 1080 us; the launch traced here: 1070 us
  other arithmetic  330 us (31%)
  blocking collectives  325 us (30%)
  waiting for transfers between devices  257 us (24%)
  local copies, waits for them, and re-layouts  76.1 us (7%)
  matrix products  52.6 us (5%)
  between operations  14.9 us (1%)
  starting transfers between devices  14.6 us (1%)
    reduce_sum x32, other arithmetic, operator_block(): return jnp.sum(jnp.where(match, weights[:, :, None], 0.0), axis=1)  256 us
    psum x3, blocking collectives, global_sum(): return lax.psum(value, ('row', 'col'))  196 us
    all_gather x2, blocking collectives, collect(): return lax.all_gather(columns, ('row', 'col'), axis=1, tiled=True)  129 us
    ppermute x4, waiting for transfers between devices, shards(): lax.ppermute(w_next[-1] if w_next else snapshots, axis_name='row', perm=r...  88.1 us
    reduce_scatter x1, waiting for transfers between devices, shards(): lax.psum_scatter(jnp.where(keep, term, 0.0).astype(jnp.bfloat16), 'col',...  85 us
    psum x1, waiting for transfers between devices, shards(): slot_kernel = lax.psum(kernel_part, 'col')  83.3 us
    dot_general x3, matrix products, apply_rows(): lax.dot_general(basis_rows, transition, (((1,), (1,)), ((), ())), precisi...  27.7 us
    unnamed x30, local copies, waits for them, and re-layouts  25.8 us
  transfers between devices with their start and end apart: 9, of which 7 were waited for; matrix products, arithmetic and copies ran while one was open for 1% of the time, Pallas kernels for 0%

profile of v1, /device:TPU:1, one launch (start us, length us, event | category | flops | bytes accessed | tf_op | source)
XLA Modules:
  0.0 1071.2 jit_solution(553689574083091835)
XLA Ops:
  10.3 23.3 %collective-permute-done = bf16[512,2048]{1,0:T(8,128)(2,1)S(1)} collective-permute-done((bf16[512,2048]{1,0:T(8,128)(2,1)}, bf16[512,2048]{1,0:T(8,128)(2,1)S(1)}, u32[]{:S(2)}, u32[]{:S(2)}) %collective-permute-start) | collective-permute-done | bytes 2097184 | tf_op jit(solution)/shard_map/ppermute | solution.py:38
  36.2 22.8 %collective-permute-done.1 = bf16[512,2048]{1,0:T(8,128)(2,1)S(1)} collective-permute-done((bf16[512,2048]{1,0:T(8,128)(2,1)S(1)}, bf16[512,2048]{1,0:T(8,128)(2,1)S(1)}, u32[]{:S(2)}, u32[]{:S(2)}) %collective-permute-start.1) | collective-permute-done | bytes 2097184 | tf_op jit(solution)/shard_map/ppermute | solution.py:38
  64.1 21.5 %collective-permute-done.2 = bf16[512,2048]{1,0:T(8,128)(2,1)} collective-permute-done((bf16[512,2048]{1,0:T(8,128)(2,1)S(1)}, bf16[512,2048]{1,0:T(8,128)(2,1)}, u32[]{:S(2)}, u32[]{:S(2)}) %collective-permute-start.2) | collective-permute-done | bytes 2097184 | tf_op jit(solution)/shard_map/ppermute | solution.py:38
  91.0 20.5 %collective-permute-done.3 = bf16[512,2048]{1,0:T(8,128)(2,1)} collective-permute-done((bf16[512,2048]{1,0:T(8,128)(2,1)}, bf16[512,2048]{1,0:T(8,128)(2,1)}, u32[]{:S(2)}, u32[]{:S(2)}) %collective-permute-start.3) | collective-permute-done | bytes 2097184 | tf_op jit(solution)/shard_map/ppermute | solution.py:38
  126.0 8.0 gather_fusion
  141.6 8.0 gather_fusion.1
  167.3 21.4 %fusion.5 = bf16[16,320,2048]{2,1,0:T(8,128)(2,1)} fusion(bf16[15,64,2048]{2,1,0:T(8,128)(2,1)S(1)} %slice.73, bf16[16,256,2048]{2,1,0:T(8,128)(2,1)} %bitcast.85), kind=kLoop, calls=%fused_computation.17 | loop fusion | flops 62914560 | bytes 41680896 | tf_op jit(solution)/shard_map/concatenate | solution.py:69
  188.9 23.8 %select_convert_fusion = bf16[5120,576]{1,0:T(8,128)(2,1)} fusion(bf16[5120,2048]{1,0:T(8,128)(2,1)} %bitcast.92, f32[576]{0:T(1024)S(1)} %pad_dynamic-slice_fusion.2, f32[5120]{0:T(1024)S(1)} %add.156, pred[576]{0:T(1024)(128)(4,1)S(1)} %add_compare_fusion, pred[5120]{0:T(1024)(128)(4,1)S(1)} %fusion.17, s32[]{:T(128)S(6)} %select_n.81, ...), kind=kOutput, calls=%fused_computation.19 | convolution fusion | flops 12097290240 | bytes 43675460 | tf_op jit(solution)/shard_map/dot_general | solution.py:77
  213.0 85.0 %reduce-scatter.2.cloned.1.call-done = bf16[320,576]{1,0:T(8,128)(2,1)} async-done(((bf16[5120,576]{1,0:T(8,128)(2,1)}), bf16[320,576]{1,0:T(8,128)(2,1)}) %reduce-scatter.2.cloned.1.call-update) | async-done | bytes 368656 | tf_op jit(solution)/shard_map/reduce_scatter | solution.py:82
  301.2 27.6 %while.22 = (s32[]{:T(128)}, f32[32,16,128]{2,1,0:T(8,128)S(1)}, s32[32,16,128]{2,1,0:T(8,128)S(1)}, f32[32,16,256]{2,1,0:T(8,128)S(1)}, s32[]{:T(128)}) while((s32[]{:T(128)}, f32[32,16,128]{2,1,0:T(8,128)S(1)}, s32[32,16,128]{2,1,0:T(8,128)S(1)}, f32[32,16,256]{2,1,0:T(8,128)S(1)}, s32[]{:T(128)}) %tuple.62), condition=%wide.region_4.5_spmd.clone, body=%wide.region_2.4_spmd.clone.sunk | while | flops 1570818 | bytes 98377 | solution.py:102
  329.7 83.3 %all-reduce.6.cloned.1.call-done = f32[512,128]{1,0:T(8,128)} async-done(((f32[512,128]{1,0:T(8,128)}), f32[512,128]{1,0:T(8,128)}) %all-reduce.6.cloned.1.call-update) | async-done | bytes 262160 | tf_op jit(solution)/shard_map/psum | solution.py:111
  415.2 280.2 %while.23 = (s32[]{:T(128)}, f32[32,16,4096]{2,1,0:T(8,128)}, s32[32,16,128]{2,1,0:T(8,128)S(1)}, f32[32,16,128]{2,1,0:T(8,128)S(1)}, s32[]{:T(128)}) while((s32[]{:T(128)}, f32[32,16,4096]{2,1,0:T(8,128)}, s32[32,16,128]{2,1,0:T(8,128)S(1)}, f32[32,16,128]{2,1,0:T(8,128)S(1)}, s32[]{:T(128)}) %tuple.63), condition=%wide.region_9.10_spmd.clone, body=%wide.region_7.9_spmd.clone.sunk | while | flops 25100288 | bytes 836165 | solution.py:121
  424.0 8.0 select_reduce_fusion.6
  432.8 8.0 select_reduce_fusion.6
  441.5 8.0 select_reduce_fusion.6
  450.3 8.0 select_reduce_fusion.6
  459.0 8.0 select_reduce_fusion.6
  467.8 8.0 select_reduce_fusion.6
  476.5 8.0 select_reduce_fusion.6
  485.3 8.0 select_reduce_fusion.6
  494.1 8.0 select_reduce_fusion.6
  502.8 8.0 select_reduce_fusion.6
  511.6 8.0 select_reduce_fusion.6
  520.3 8.0 select_reduce_fusion.6
  529.1 8.0 select_reduce_fusion.6
  537.9 8.0 select_reduce_fusion.6
  546.6 8.0 select_reduce_fusion.6
  555.4 8.0 select_reduce_fusion.6
  564.1 8.0 select_reduce_fusion.6
  572.8 8.0 select_reduce_fusion.6
  581.6 8.0 select_reduce_fusion.6
  590.4 8.0 select_reduce_fusion.6
  599.1 8.0 select_reduce_fusion.6
  607.9 8.0 select_reduce_fusion.6
  616.6 8.0 select_reduce_fusion.6
  625.4 8.0 select_reduce_fusion.6
  634.2 8.0 select_reduce_fusion.6
  651.7 8.0 select_reduce_fusion.6
  660.4 8.0 select_reduce_fusion.6
  669.2 8.0 select_reduce_fusion.6
  695.4 9.2 fusion.49
  704.9 65.8 %psum.29 = f32[32,32]{0,1:T(8,128)S(1)} all-reduce(f32[32,32]{0,1:T(8,128)S(1)} %fusion.36), channel_id=1, replica_groups=mesh['row'=8,'col'=16] {'row','col'}, use_global_device_ids=true, to_apply=%region_10.11 | all-reduce | flops 1024 | bytes 8192 | tf_op jit(solution)/shard_map/psum | solution.py:19
  777.6 63.7 %all_gather.6 = f32[32,4096]{0,1:T(8,128)S(1)} all-gather(f32[32,32]{0,1:T(8,128)S(1)} %fusion.23), channel_id=1, replica_groups=mesh['row'=8,'col'=16] {'row','col'}, dimensions={1}, use_global_device_ids=true | all-gather | bytes 528384 | tf_op jit(solution)/shard_map/all_gather | solution.py:23
  841.3 9.3 fusion.50
  850.8 65.0 %psum.30 = f32[32,32]{0,1:T(8,128)S(1)} all-reduce(f32[32,32]{0,1:T(8,128)S(1)} %fusion.33), channel_id=1, replica_groups=mesh['row'=8,'col'=16] {'row','col'}, use_global_device_ids=true, to_apply=%region_13.16 | all-reduce | flops 1024 | bytes 8192 | tf_op jit(solution)/shard_map/psum | solution.py:19
  922.9 65.1 %all_gather.7 = f32[32,4096]{0,1:T(8,128)S(1)} all-gather(f32[32,32]{0,1:T(8,128)S(1)} %fusion.20), channel_id=1, replica_groups=mesh['row'=8,'col'=16] {'row','col'}, dimensions={1}, use_global_device_ids=true | all-gather | bytes 528384 | tf_op jit(solution)/shard_map/all_gather | solution.py:23
  988.1 9.3 fusion.51
  997.6 65.0 %psum.31 = f32[32,32]{0,1:T(8,128)S(1)} all-reduce(f32[32,32]{0,1:T(8,128)S(1)} %fusion.29), channel_id=1, replica_groups=mesh['row'=8,'col'=16] {'row','col'}, use_global_device_ids=true, to_apply=%region_14.17 | all-reduce | flops 1024 | bytes 8192 | tf_op jit(solution)/shard_map/psum | solution.py:19
  (325 shorter events, 160.1 us)
Async XLA Ops:
  7.2 688.3 %copy-start = (f32[32,4096]{1,0:T(8,128)S(1)}, f32[32,4096]{1,0:T(8,128)}, u32[]{:S(2)}) copy-start(f32[32,4096]{1,0:T(8,128)} %param.12) | copy-start | bytes 1572868
  7.2 290.7 %reduce-scatter.2.cloned.1.call-start = ((), (), s32[]{:S(2)}) async-start(), calls=%async_computation.1 | async-start | bytes 6963200 | tf_op jit(solution)/shard_map/reduce_scatter | solution.py:82
  7.2 26.3 %collective-permute-start = (bf16[512,2048]{1,0:T(8,128)(2,1)}, bf16[512,2048]{1,0:T(8,128)(2,1)S(1)}, u32[]{:S(2)}, u32[]{:S(2)}) collective-permute-start(bf16[512,2048]{1,0:T(8,128)(2,1)} %param.10), channel_id=1, source_target_pairs={{0,16},{16,32},{32,48},{48,64},{64,80},{80,96},{96,112},{112,0},{1... | collective-permute-start | bytes 6291464 | tf_op jit(solution)/shard_map/ppermute | solution.py:38
  33.6 25.4 %collective-permute-start.1 = (bf16[512,2048]{1,0:T(8,128)(2,1)S(1)}, bf16[512,2048]{1,0:T(8,128)(2,1)S(1)}, u32[]{:S(2)}, u32[]{:S(2)}) collective-permute-start(bf16[512,2048]{1,0:T(8,128)(2,1)S(1)} %collective-permute-done), channel_id=1, source_target_pairs={{0,16},{16,32},{32,48},{48,64},{64,80},{80,96},{96,112},{112,0},{1... | collective-permute-start | bytes 6291464 | tf_op jit(solution)/shard_map/ppermute | solution.py:38
  35.9 26.8 %collective-permute-start.4 = (bf16[512,2048]{1,0:T(8,128)(2,1)}, bf16[512,2048]{1,0:T(8,128)(2,1)}, u32[]{:S(2)}, u32[]{:S(2)}) collective-permute-start(bf16[512,2048]{1,0:T(8,128)(2,1)} %param.10), channel_id=1, source_target_pairs={{16,0},{32,16},{48,32},{64,48},{80,64},{96,80},{112,96},{0,112},{1... | collective-permute-start | bytes 6291464 | tf_op jit(solution)/shard_map/ppermute | solution.py:42
  58.9 1.3 copy-start.2
  60.2 25.5 %collective-permute-start.2 = (bf16[512,2048]{1,0:T(8,128)(2,1)S(1)}, bf16[512,2048]{1,0:T(8,128)(2,1)}, u32[]{:S(2)}, u32[]{:S(2)}) collective-permute-start(bf16[512,2048]{1,0:T(8,128)(2,1)S(1)} %collective-permute-done.1), channel_id=1, source_target_pairs={{0,16},{16,32},{32,48},{48,64},{64,80},{80,96},{96,112},{112,0},{1... | collective-permute-start | bytes 6291464 | tf_op jit(solution)/shard_map/ppermute | solution.py:38
  62.7 26.1 %collective-permute-start.5 = (bf16[512,2048]{1,0:T(8,128)(2,1)}, bf16[512,2048]{1,0:T(8,128)(2,1)}, u32[]{:S(2)}, u32[]{:S(2)}) collective-permute-start(bf16[512,2048]{1,0:T(8,128)(2,1)} %collective-permute-done.4), channel_id=1, source_target_pairs={{16,0},{32,16},{48,32},{64,48},{80,64},{96,80},{112,96},{0,112},{1... | collective-permute-start | bytes 6291464 | tf_op jit(solution)/shard_map/ppermute | solution.py:42
  85.7 25.9 %collective-permute-start.3 = (bf16[512,2048]{1,0:T(8,128)(2,1)}, bf16[512,2048]{1,0:T(8,128)(2,1)}, u32[]{:S(2)}, u32[]{:S(2)}) collective-permute-start(bf16[512,2048]{1,0:T(8,128)(2,1)} %collective-permute-done.2), channel_id=1, source_target_pairs={{0,16},{16,32},{32,48},{48,64},{64,80},{80,96},{96,112},{112,0},{1... | collective-permute-start | bytes 6291464 | tf_op jit(solution)/shard_map/ppermute | solution.py:38
  88.3 27.0 %copy-start.3 = (bf16[512,2048]{1,0:T(8,128)(2,1)S(1)}, bf16[512,2048]{1,0:T(8,128)(2,1)}, u32[]{:S(2)}) copy-start(bf16[512,2048]{1,0:T(8,128)(2,1)} %copy-done.2) | copy-start | bytes 6291460
  88.3 27.2 %copy-start.1 = (bf16[512,2048]{1,0:T(8,128)(2,1)S(1)}, bf16[512,2048]{1,0:T(8,128)(2,1)}, u32[]{:S(2)}) copy-start(bf16[512,2048]{1,0:T(8,128)(2,1)} %param.10) | copy-start | bytes 6291460
  88.8 30.6 %collective-permute-start.6 = (bf16[512,2048]{1,0:T(8,128)(2,1)}, bf16[512,2048]{1,0:T(8,128)(2,1)S(1)}, u32[]{:S(2)}, u32[]{:S(2)}) collective-permute-start(bf16[512,2048]{1,0:T(8,128)(2,1)} %collective-permute-done.5), channel_id=1, source_target_pairs={{16,0},{32,16},{48,32},{64,48},{80,64},{96,80},{112,96},{0,112},{1... | collective-permute-start | bytes 6291464 | tf_op jit(solution)/shard_map/ppermute | solution.py:42
  164.7 24.1 %slice-start = ((s8[16777216]{0:T(1024)(128)(4,1)}), s8[4194304]{0:T(1024)(128)(4,1)S(1)}, s32[]{:S(2)}) async-start(s8[16777216]{0:T(1024)(128)(4,1)} %bitcast.86), calls=%async_computation.3 | async-start | bytes 8388608
  167.3 21.6 %slice-start.1 = ((s8[16777216]{0:T(1024)(128)(4,1)}), s8[4194304]{0:T(1024)(128)(4,1)S(1)}, s32[]{:S(2)}) async-start(s8[16777216]{0:T(1024)(128)(4,1)} %bitcast.86), calls=%async_computation.4 | async-start | bytes 8388608
  167.3 21.5 %slice-start.2 = ((s8[16777216]{0:T(1024)(128)(4,1)}), s8[4194304]{0:T(1024)(128)(4,1)S(1)}, s32[]{:S(2)}) async-start(s8[16777216]{0:T(1024)(128)(4,1)} %bitcast.86), calls=%async_computation.5 | async-start | bytes 8388608
  167.3 21.5 %slice-start.3 = ((s8[16777216]{0:T(1024)(128)(4,1)}), s8[4194304]{0:T(1024)(128)(4,1)S(1)}, s32[]{:S(2)}) async-start(s8[16777216]{0:T(1024)(128)(4,1)} %bitcast.86), calls=%async_computation.6 | async-start | bytes 8388608
  188.9 24.0 %copy-start.4 = (s32[512,128]{1,0:T(8,128)S(1)}, s32[512,128]{1,0:T(8,128)}, u32[]{:S(2)}) copy-start(s32[512,128]{1,0:T(8,128)} %param.11) | copy-start | bytes 786436
  212.7 200.3 %all-reduce.6.cloned.1.call-start = ((), (), s32[]{:S(2)}) async-start(), calls=%async_computation.2 | async-start | bytes 524288 | tf_op jit(solution)/shard_map/psum | solution.py:111
Sparse Core Ops, SparseCore 0:
  212.8 85.0 reduce-scatter.1
  329.8 83.1 all-reduce.5
